TPU v7x, 512 devices: a whole 4x8x8 slice. The times are simulated.
512 devices in a mesh: wide: 128 (over y, z, core), pair: 4 (over x).
Axes of the slice: x: 4, y: 8, z: 8, core: 2. Of those that a mesh axis runs over, the one named last changes fastest.
Arguments:
- blocks: bfloat16 [2048, 1024, 512], P('pair', 'wide'), may hold values from -6 to 6
- basis_a: bfloat16 [1024, 64], replicated, may hold values from -0.1875 to 0.1875
- basis_b: bfloat16 [512, 64], replicated, may hold values from -0.25 to 0.25
- sketch: bfloat16 [2048, 64], P(('pair', 'wide')), may hold values from -6 to 6
Outputs:
- transfer: float32 [4096, 64], P(('wide', 'pair'))
- coefficients: float32 [2048, 64], P(('pair', 'wide'))
All inputs are finite; a program needn't handle non-finite values.
Results may differ from a plain program's by a relative error of at most 0.0041.
Values may be sent and summed in bfloat16 or wider, within the bound.
A program may use at most 64 MiB of HBM per device.

v0:
```python
import jax
import jax.numpy as jnp
from jax import lax
from jax.sharding import PartitionSpec as P


def orthonormal(sketched, gram):
    lower = jnp.linalg.cholesky(gram)
    return lax.linalg.triangular_solve(
        lower, sketched, left_side=False, lower=True, transpose_a=True
    )


def per_device(blocks, basis_a, basis_b, sketch):
    fibres = sketch.shape[0]
    rank_a = basis_a.shape[1]
    rank_b = basis_b.shape[1]
    narrowed = jnp.einsum(
        "fac,cr->far", blocks, basis_b, preferred_element_type=jnp.float32
    ).astype(jnp.bfloat16)
    regrouped = lax.all_to_all(narrowed, "wide", split_axis=0, concat_axis=1, tiled=True)
    projected = jnp.einsum(
        "ap,far->fpr", basis_a, regrouped, preferred_element_type=jnp.float32
    ).astype(jnp.bfloat16)
    projected = projected.reshape(fibres, rank_a * rank_b)
    partial_value = jnp.einsum("fj,fk->jk", projected, sketch, preferred_element_type=jnp.float32)
    own_count = rank_a * rank_b // lax.axis_size(("wide", "pair"))
    sketch_all = lax.psum(partial_value, ("wide", "pair"))
    gram_matrix = jnp.dot(sketch_all.T, sketch_all, precision=lax.Precision.HIGHEST)
    parent_basis = orthonormal(sketch_all, gram_matrix)
    first_row = lax.axis_index(("wide", "pair")) * own_count
    own_basis = lax.dynamic_slice_in_dim(parent_basis, first_row, own_count, 0)
    transfer = own_basis * jnp.sqrt(jnp.float32(rank_a * rank_b))
    coefficients = jnp.dot(
        projected.astype(jnp.float32), parent_basis, precision=lax.Precision.HIGHEST
    )
    return (transfer, coefficients)


def solution(mesh):
    placed = (P("pair", "wide", None), P(), P(), P(("pair", "wide"), None))
    return jax.shard_map(
        per_device,
        mesh=mesh,
        in_specs=placed,
        out_specs=(P(("wide", "pair"), None), P(("pair", "wide"), None)),
        check_vma=False,
    )
```

profile of v0, /device:TPU:24, one launch (start us, length us, event | category | flops | bytes accessed | tf_op | source)
XLA Modules:
  0.0 346.8 jit_solution(4763148819996868437)
XLA Ops:
  7.2 0.0 copy-start
  7.2 0.0 all-reduce.2.cloned.1.call-start
  7.2 3.4 convolution_convert_fusion
  10.7 0.0 copy-start.1
  10.7 0.6 reshape.19
  11.3 35.6 %all_to_all.18 = bf16[128,2,1024]{2,1,0:T(2,128)(2,1)S(1)} all-to-all(bf16[128,2,1024]{2,1,0:T(2,128)(2,1)S(1)} %reshape.19), channel_id=1, replica_groups=mesh['wide'=128,'pair'=4] {'wide'}, dimensions={0} | all-to-all | bytes 1048576 | tf_op jit(solution)/shard_map/all_to_all | solution.py:21
  46.9 0.6 reshape.20
  47.5 0.0 copy-done
  47.5 0.5 fusion
  48.0 0.1 copy.19
  48.1 0.1 reshape.16
  48.2 1.4 fusion.9
  49.6 0.0 all-reduce.2.cloned.1.call-update
  49.6 271.4 %all-reduce.2.cloned.1.call-done = f32[4096,64]{0,1:T(8,128)} async-done(((f32[4096,64]{0,1:T(8,128)}), f32[4096,64]{0,1:T(8,128)}) %all-reduce.2.cloned.1.call-update) | async-done | bytes 1048592 | tf_op jit(solution)/shard_map/psum | solution.py:28
  321.0 2.5 fusion.10
  323.5 0.1 copy.20
  323.6 5.8 %cholesky.16 = f32[64,64]{1,0:T(8,128)S(1)} custom-call(f32[64,64]{1,0:T(8,128)S(1)} %fusion.8), custom_call_target="Cholesky" | custom-call | tf_op jit(solution)/shard_map/jit(cholesky)/cholesky | solution.py:8
  329.5 0.6 compare_reduce_fusion
  330.2 0.7 fusion.5
  330.8 4.9 %custom-call.6 = f32[1,64,64]{1,2,0:T(8,128)S(1)} custom-call(f32[1,64,64]{2,1,0:T(8,128)S(1)} %fusion.5), custom_call_target="InvertDiagBlocksLowerTriangular" | custom-call | tf_op jit(solution)/shard_map/triangular_solve | solution.py:9
  335.7 2.3 fusion.6
  338.0 1.2 fusion.11
  339.2 0.1 dynamic-slice_multiply_fusion
  339.3 0.7 copy.21
  (3 shorter events, 0.0 us)
Async XLA Ops:
  7.2 40.3 %copy-start = (bf16[1024,64]{0,1:T(8,128)(2,1)S(1)}, bf16[1024,64]{0,1:T(8,128)(2,1)}, u32[]{:S(2)}) copy-start(bf16[1024,64]{0,1:T(8,128)(2,1)} %param.5) | copy-start | bytes 393220
  7.2 313.8 %all-reduce.2.cloned.1.call-start = ((), (), s32[]{:S(2)}) async-start(), calls=%async_computation.1 | async-start | bytes 2097152 | tf_op jit(solution)/shard_map/psum | solution.py:28
  10.7 37.5 %copy-start.1 = (bf16[4,64]{1,0:T(4,128)(2,1)S(1)}, bf16[4,64]{1,0:T(4,128)(2,1)}, u32[]{:S(2)}) copy-start(bf16[4,64]{1,0:T(4,128)(2,1)} %param.7) | copy-start | bytes 1540
Sparse Core Ops, SparseCore 0:
  49.7 271.2 all-reduce.1
where the time goes:
time: 347 us
  waiting for transfers between devices  271 us (78%)
  blocking collectives  35.6 us (10%)
  between operations  14.1 us (4%)
  other arithmetic  12.2 us (4%)
  matrix products  11.3 us (3%)
    psum x1, waiting for transfers between devices, per_device(): sketch_all = lax.psum(partial_value, ('wide', 'pair'))  271 us
    all_to_all x1, blocking collectives, per_device(): lax.all_to_all(narrowed, 'wide', split_axis=0, concat_axis=1, tiled=True)  35.6 us
  transfers between devices with their start and end apart: 1, of which 1 were waited for; matrix products, arithmetic and copies ran while one was open for 0% of the time, Pallas kernels for 0%

commit v1 on v0

--- a/solution.py
+++ b/solution.py
@@ -25,7 +25,7 @@
     projected = projected.reshape(fibres, rank_a * rank_b)
     partial_value = jnp.einsum("fj,fk->jk", projected, sketch, preferred_element_type=jnp.float32)
     own_count = rank_a * rank_b // lax.axis_size(("wide", "pair"))
-    sketch_all = lax.psum(partial_value, ("wide", "pair"))
+    sketch_all = lax.psum(lax.psum(partial_value, "pair"), "wide")
     gram_matrix = jnp.dot(sketch_all.T, sketch_all, precision=lax.Precision.HIGHEST)
     parent_basis = orthonormal(sketch_all, gram_matrix)
     first_row = lax.axis_index(("wide", "pair")) * own_count

time: 347 us -> 330 us (0.951)
  waiting for transfers between devices: 271 us -> 255 us
    psum x1 -> x2, waiting for transfers between devices: 271 us -> 255 us  [per_device(): sketch_all = lax.psum(lax.psum(partial_value, 'pair'), 'wide')]
  transfers between devices with their start and end apart: 1 -> 2, of which waited for: 1 -> 2; matrix products, arithmetic and copies ran while one was open for 0% -> 0% of each run, Pallas kernels for 0% -> 0%
where the time goes in v1:
time: 330 us
  waiting for transfers between devices  255 us (77%)
  blocking collectives  35.6 us (11%)
  between operations  14.2 us (4%)
  other arithmetic  12.2 us (4%)
  matrix products  11.4 us (3%)
    psum x2, waiting for transfers between devices, per_device(): sketch_all = lax.psum(lax.psum(partial_value, 'pair'), 'wide')  255 us
    all_to_all x1, blocking collectives, per_device(): lax.all_to_all(narrowed, 'wide', split_axis=0, concat_axis=1, tiled=True)  35.6 us
  transfers between devices with their start and end apart: 2, of which 2 were waited for; matrix products, arithmetic and copies ran while one was open for 0% of the time, Pallas kernels for 0%

profile of v1, /device:TPU:24, one launch (start us, length us, event | category | flops | bytes accessed | tf_op | source)
XLA Modules:
  0.0 330.1 jit_solution(7173992547782186564)
XLA Ops:
  7.2 0.0 all-reduce.3.cloned.1.call-start
  7.2 3.4 %convolution_convert_fusion = bf16[512,8,64]{2,1,0:T(8,128)(2,1)S(1)} fusion(bf16[512,8,512]{2,1,0:T(8,128)(2,1)} %param.4, bf16[512,64]{0,1:T(8,128)(2,1)} %param.6), kind=kOutput, calls=%fused_computation | convolution fusion | flops 268697600 | bytes 4784128 | tf_op jit(solution)/shard_map/fac,cr->far/dot_general | solution.py:18
  10.7 0.6 reshape.19
  11.3 35.6 %all_to_all.18 = bf16[128,2,1024]{2,1,0:T(2,128)(2,1)S(1)} all-to-all(bf16[128,2,1024]{2,1,0:T(2,128)(2,1)S(1)} %reshape.19), channel_id=1, replica_groups=mesh['wide'=128,'pair'=4] {'wide'}, dimensions={0} | all-to-all | bytes 1048576 | tf_op jit(solution)/shard_map/all_to_all | solution.py:21
  46.9 0.6 reshape.20
  47.5 0.5 fusion
  48.0 0.1 copy.19
  48.1 0.1 reshape.16
  48.2 1.4 fusion.9
  49.6 0.0 all-reduce.3.cloned.1.call-update
  49.6 0.0 all-reduce.5.cloned.1.call-start
  49.7 51.4 %all-reduce.3.cloned.1.call-done = f32[4096,64]{0,1:T(8,128)} async-done(((f32[4096,64]{0,1:T(8,128)}), f32[4096,64]{0,1:T(8,128)}) %all-reduce.3.cloned.1.call-update) | async-done | bytes 1048592 | tf_op jit(solution)/shard_map/psum | solution.py:28
  101.0 0.0 all-reduce.5.cloned.1.call-update
  101.1 203.2 %all-reduce.5.cloned.1.call-done = f32[4096,64]{0,1:T(8,128)} async-done(((f32[4096,64]{0,1:T(8,128)}), f32[4096,64]{0,1:T(8,128)}) %all-reduce.5.cloned.1.call-update) | async-done | bytes 1048592 | tf_op jit(solution)/shard_map/psum | solution.py:28
  304.2 2.6 fusion.10
  306.9 0.1 copy.20
  307.0 5.8 %cholesky.16 = f32[64,64]{1,0:T(8,128)S(1)} custom-call(f32[64,64]{1,0:T(8,128)S(1)} %fusion.8), custom_call_target="Cholesky" | custom-call | tf_op jit(solution)/shard_map/jit(cholesky)/cholesky | solution.py:8
  312.9 0.6 compare_reduce_fusion
  313.5 0.7 fusion.5
  314.2 4.9 %custom-call.6 = f32[1,64,64]{1,2,0:T(8,128)S(1)} custom-call(f32[1,64,64]{2,1,0:T(8,128)S(1)} %fusion.5), custom_call_target="InvertDiagBlocksLowerTriangular" | custom-call | tf_op jit(solution)/shard_map/triangular_solve | solution.py:9
  319.1 2.3 fusion.6
  321.3 1.2 fusion.11
  322.5 0.1 dynamic-slice_multiply_fusion
  322.6 0.7 copy.21
  (6 shorter events, 0.1 us)
Async XLA Ops:
  7.2 40.3 %copy-start = (bf16[1024,64]{0,1:T(8,128)(2,1)S(1)}, bf16[1024,64]{0,1:T(8,128)(2,1)}, u32[]{:S(2)}) copy-start(bf16[1024,64]{0,1:T(8,128)(2,1)} %param.5) | copy-start | bytes 393220
  7.2 93.8 %all-reduce.3.cloned.1.call-start = ((), (), s32[]{:S(2)}) async-start(), calls=%async_computation.1 | async-start | bytes 2097152 | tf_op jit(solution)/shard_map/psum | solution.py:28
  10.7 37.5 %copy-start.1 = (bf16[4,64]{1,0:T(4,128)(2,1)S(1)}, bf16[4,64]{1,0:T(4,128)(2,1)}, u32[]{:S(2)}) copy-start(bf16[4,64]{1,0:T(4,128)(2,1)} %param.7) | copy-start | bytes 1540
  49.6 254.6 %all-reduce.5.cloned.1.call-start = ((), (), s32[]{:S(2)}) async-start(), calls=%async_computation.2 | async-start | bytes 2097152 | tf_op jit(solution)/shard_map/psum | solution.py:28
Sparse Core Ops, SparseCore 0:
  49.7 51.2 all-reduce.2
  104.3 199.9 all-reduce.4
